TPU v7x, 512 devices: a whole 4x8x8 slice. The times are simulated.
512 devices in a mesh: ep: 8 (over y), etp: 64 (over z, x, core).
Axes of the slice: x: 4, y: 8, z: 8, core: 2. Of those that a mesh axis runs over, the one named last changes fastest.
Arguments:
- tokens: bfloat16 [384, 3072], P('ep', 'etp'), may hold values from -6 to 6
- routes: int32 [384, 2], P('ep'), may hold values from 0 to 7, as said below
- route_gates: float32 [384, 2], P('ep'), may hold values from 0.1 to 0.9
- cotangent: bfloat16 [384, 3072], P('ep', 'etp'), may hold values from -1.5 to 1.5
- w_gate: bfloat16 [8, 3072, 8192], P('ep', None, 'etp'), may hold values from -0.109375 to 0.109375
- w_up: bfloat16 [8, 3072, 8192], P('ep', None, 'etp'), may hold values from -0.109375 to 0.109375
- w_down: bfloat16 [8, 8192, 3072], P('ep', 'etp'), may hold values from -0.1875 to 0.1875
Outputs:
- mixed: bfloat16 [384, 3072], P('ep', 'etp')
- grad_gates: float32 [384, 2], P('ep')
- grad_w_gate: bfloat16 [8, 3072, 8192], P('ep', None, 'etp')
- grad_w_up: bfloat16 [8, 3072, 8192], P('ep', None, 'etp')
- grad_w_down: bfloat16 [8, 8192, 3072], P('ep', 'etp')
Inputs may be any that keep to these rules, and one draw needn't show every extreme that they name: `routes`: within each aligned block of 48 rows (the tokens of one index of ep) the two experts of a row differ and no expert is named by more than 24 rows; one expert, the same in every block, is named by exactly 24 rows of each block.
All inputs are finite; a program needn't handle non-finite values.
Results may differ from a plain program's by a relative error of at most 0.0058.
Values may be sent and summed in bfloat16 or wider, within the bound.
A program may use at most 64 MiB of HBM per device.

v0:
```python
import jax
import jax.numpy as jnp
from jax import lax
from jax.sharding import PartitionSpec as P

EXPERTS = 8
CAP = 24


def per_device(tokens, routes, route_gates, cotangent, w_gate, w_up, w_down):
    local_experts = w_gate.shape[0]
    ep_count = lax.axis_size("ep")
    tok_count = tokens.shape[0]
    flat_ids = routes.reshape(-1)
    pair_count = flat_ids.shape[0]
    onehot = (flat_ids[:, None] == jnp.arange(EXPERTS, dtype=jnp.int32)[None, :]).astype(jnp.int32)
    before = jnp.cumsum(onehot, axis=0) - onehot
    slot_id = jnp.sum(before * onehot, axis=1)
    target = flat_ids * CAP + slot_id
    slot_table = (
        jnp.full((EXPERTS * CAP,), pair_count, jnp.int32)
        .at[target]
        .set(jnp.arange(pair_count, dtype=jnp.int32))
    )
    token_of_slot = slot_table // 2
    gate_flat = jnp.concatenate([route_gates.reshape(-1), jnp.zeros((1,), jnp.float32)])
    slot_gate = gate_flat[slot_table][:, None]
    gates_wide = route_gates[:, :, None]
    width = tokens.shape[1]
    x_pad = jnp.concatenate([tokens, jnp.zeros((1, width), jnp.bfloat16)], axis=0)
    dy_pad = jnp.concatenate([cotangent, jnp.zeros((1, width), jnp.bfloat16)], axis=0)
    x_sent = x_pad[token_of_slot].reshape(ep_count, local_experts, CAP, width)
    dy_rows = (slot_gate * dy_pad[token_of_slot].astype(jnp.float32)).astype(jnp.bfloat16)
    x_sent, dy_sent = (x_sent, dy_rows.reshape(ep_count, local_experts, CAP, width))
    x_recv, dy_recv = (
        lax.all_to_all(x_sent, "ep", split_axis=0, concat_axis=2, tiled=True),
        lax.all_to_all(dy_sent, "ep", split_axis=0, concat_axis=2, tiled=True),
    )
    x_rows, dy_rows = (
        lax.all_gather(x_recv, "etp", axis=3, tiled=True),
        lax.all_gather(dy_recv, "etp", axis=3, tiled=True),
    )
    rows_x = x_rows[0]
    rows_dy = dy_rows[0]
    gate_pre = jnp.einsum("erd,edf->erf", rows_x, w_gate, preferred_element_type=jnp.float32)
    up_pre = jnp.einsum("erd,edf->erf", rows_x, w_up, preferred_element_type=jnp.float32)
    sigma = jax.nn.sigmoid(gate_pre)
    hidden = (jax.nn.silu(gate_pre) * up_pre).astype(jnp.bfloat16)
    output_part = jnp.einsum("erf,efd->erd", hidden, w_down, preferred_element_type=jnp.float32)
    d_hidden = jnp.einsum("erd,efd->erf", rows_dy, w_down, preferred_element_type=jnp.float32)
    d_up = (d_hidden * jax.nn.silu(gate_pre)).astype(jnp.bfloat16)
    d_gate = (d_hidden * up_pre * sigma * (1.0 + gate_pre * (1.0 - sigma))).astype(jnp.bfloat16)
    grad_down = jnp.einsum("erf,erd->efd", hidden, rows_dy, preferred_element_type=jnp.float32)
    grad_gate_w = jnp.einsum("erd,erf->edf", rows_x, d_gate, preferred_element_type=jnp.float32)
    grad_up_w = jnp.einsum("erd,erf->edf", rows_x, d_up, preferred_element_type=jnp.float32)
    output_part, grad_w_gate, grad_w_up, grad_w_down = (
        output_part,
        grad_gate_w.astype(jnp.bfloat16),
        grad_up_w.astype(jnp.bfloat16),
        grad_down.astype(jnp.bfloat16),
    )
    returned = lax.all_to_all(output_part[None], "ep", split_axis=2, concat_axis=0, tiled=True)
    pair_rows = returned.reshape(EXPERTS * CAP, -1)[target].reshape(tok_count, 2, -1)
    full_rows = lax.psum_scatter(pair_rows, "etp", scatter_dimension=2, tiled=True)
    mixed = jnp.sum(gates_wide * full_rows, axis=1).astype(jnp.bfloat16)
    partial_grad = jnp.sum(full_rows * cotangent.astype(jnp.float32)[:, None, :], axis=2)
    grad_gates = lax.psum(partial_grad, "etp")
    return (mixed, grad_gates, grad_w_gate, grad_w_up, grad_w_down)


def solution(mesh):
    in_specs = (
        P("ep", "etp"),
        P("ep", None),
        P("ep", None),
        P("ep", "etp"),
        P("ep", None, "etp"),
        P("ep", None, "etp"),
        P("ep", "etp", None),
    )
    out_specs = (
        P("ep", "etp"),
        P("ep", None),
        P("ep", None, "etp"),
        P("ep", None, "etp"),
        P("ep", "etp", None),
    )
    return jax.shard_map(
        per_device, mesh=mesh, in_specs=in_specs, out_specs=out_specs, check_vma=False
    )
```

profile of v0, /device:TPU:8, one launch (start us, length us, event | category | flops | bytes accessed | tf_op | source)
XLA Modules:
  0.0 672.6 jit_solution(16049948253081429663)
XLA Ops:
  7.2 0.0 all-gather.3.cloned.1.call-start
  7.2 0.8 broadcast_multiply_fusion
  8.0 0.8 copy.22
  8.8 0.1 copy.21
  8.9 0.1 mul.85
  9.0 0.1 eq.15
  9.1 0.1 fusion.19
  9.2 0.1 reduce_window_sum.11
  9.4 0.2 select_reduce_fusion
  9.6 0.9 scatter_custom_fusion
  10.5 0.7 concatenate.9
  11.2 0.8 gather_fusion
  12.0 0.1 reshape.210
  12.1 14.6 %all_to_all.33 = bf16[8,2,576]{2,1,0:T(2,128)(2,1)S(1)} all-to-all(bf16[8,2,576]{2,1,0:T(2,128)(2,1)S(1)} %reshape.210), channel_id=1, replica_groups=mesh['ep'=8,'etp'=64] {'ep'}, dimensions={0} | all-to-all | bytes 36864 | tf_op jit(solution)/shard_map/all_to_all | solution.py:36
  26.7 0.1 reshape.211
  26.8 0.7 copy.24
  27.5 0.8 copy.20
  28.3 0.7 concatenate.11
  29.0 0.8 gather_fusion.3
  29.8 0.1 reshape.159
  29.9 0.1 pad_maximum_fusion
  30.0 1.6 gather_fusion.2
  31.6 0.1 mul.92
  31.6 0.1 fusion.16
  31.7 0.7 reshape.212
  32.5 4.6 all-to-all-start.2
  37.1 73.1 %all-gather.3.cloned.1.call-done = bf16[1,1,192,3072]{2,3,1,0:T(8,128)(2,1)} async-done(((bf16[1,1,192,48]{2,3,1,0:T(8,128)(2,1)}), bf16[1,1,192,3072]{2,3,1,0:T(8,128)(2,1)}) %all-gather.3.cloned.1.call-update) | async-done | bytes 1179664 | tf_op jit(solution)/shard_map/all_gather | solution.py:40
  110.2 2.1 fusion.10
  112.4 0.6 multiply_convert_fusion.2
  113.0 0.5 convolution_bitcast_fusion
  113.5 3.8 copy.25
  117.3 7.4 %all-to-all-start.1 = ((f32[1,1,192,3072]{3,1,0,2:T(1,128)}), f32[1,1,192,3072]{3,1,0,2:T(1,128)}, u32[]{:S(2)}, u32[]{:S(2)}) async-start(f32[1,1,192,3072]{3,1,0,2:T(1,128)} %copy.25), calls=%async_computation.1 | async-start | bytes 4718592 | tf_op jit(solution)/shard_map/all_to_all | solution.py:62
  124.7 0.1 reshape.213
  124.8 0.7 copy.28
  125.5 0.0 all-reduce.5.cloned.1.call-start
  125.6 1.3 dynamic-slice
  127.6 82.1 %all-gather.5.cloned.1.call-done = bf16[1,1,192,3072]{2,3,1,0:T(8,128)(2,1)} async-done(((bf16[1,1,192,48]{2,3,1,0:T(8,128)(2,1)}), bf16[1,1,192,3072]{2,3,1,0:T(8,128)(2,1)}) %all-gather.5.cloned.1.call-update) | async-done | bytes 1179664 | tf_op jit(solution)/shard_map/all_gather | solution.py:41
  209.7 2.0 fusion.4
  211.7 2.1 copy.34
  213.8 2.0 gather_fusion.1
  215.8 2.9 reshape.158
  218.7 3.1 fusion.2
  221.8 1.5 fusion.1
  223.3 1.5 fusion
  224.7 189.6 %all-reduce.5.cloned.1.call-done = f32[48,2,3072]{2,1,0:T(2,128)} async-done(((f32[48,2,3072]{2,1,0:T(2,128)}), f32[48,2,3072]{2,1,0:T(2,128)}) %all-reduce.5.cloned.1.call-update) | async-done | bytes 1179664
  414.3 1.7 multiply_reduce_fusion
  416.1 249.4 %psum.7 = f32[48,2]{1,0:T(8,128)S(1)} all-reduce(f32[48,2]{1,0:T(8,128)S(1)} %get-tuple-element.10), channel_id=1, replica_groups=mesh['ep'=8,'etp'=64] {'etp'}, use_global_device_ids=true, to_apply=%region_6.7 | all-reduce | flops 96 | bytes 768 | tf_op jit(solution)/shard_map/psum | solution.py:67
  665.4 0.6 copy.29
  (24 shorter events, 0.1 us)
Async XLA Ops:
  7.2 105.8 %copy-start = (bf16[1,128,3072]{2,1,0:T(8,128)(2,1)S(1)}, bf16[1,128,3072]{2,1,0:T(8,128)(2,1)}, u32[]{:S(2)}) copy-start(bf16[1,128,3072]{2,1,0:T(8,128)(2,1)} %param.13) | copy-start | bytes 2359300
  7.2 103.0 %copy-start.3 = (bf16[1,3072,128]{2,1,0:T(8,128)(2,1)S(1)}, bf16[1,3072,128]{2,1,0:T(8,128)(2,1)}, u32[]{:S(2)}) copy-start(bf16[1,3072,128]{2,1,0:T(8,128)(2,1)} %param.11) | copy-start | bytes 2359300
  7.2 103.0 %all-gather.3.cloned.1.call-start = ((), (), s32[]{:S(2)}) async-start(), calls=%async_computation.3 | async-start | bytes 1597440 | tf_op jit(solution)/shard_map/all_gather | solution.py:40
  31.5 80.8 %copy-start.5 = (bf16[1,3072,128]{2,1,0:T(8,128)(2,1)S(1)}, bf16[1,3072,128]{2,1,0:T(8,128)(2,1)}, u32[]{:S(2)}) copy-start(bf16[1,3072,128]{2,1,0:T(8,128)(2,1)} %param.12) | copy-start | bytes 2359300
  32.5 84.8 %all-to-all-start.2 = ((bf16[8,2,576]{2,1,0:T(2,128)(2,1)}), bf16[8,2,576]{2,1,0:T(2,128)(2,1)S(1)}, u32[]{:S(2)}, u32[]{:S(2)}) async-start(bf16[8,2,576]{2,1,0:T(2,128)(2,1)} %reshape.212), calls=%async_computation.2 | async-start | bytes 40960 | tf_op jit(solution)/shard_map/all_to_all | solution.py:37
  110.2 2.1 copy-start.1
  117.3 8.3 %copy-start.4 = (bf16[48,48]{1,0:T(8,128)(2,1)S(1)}, bf16[48,48]{1,0:T(8,128)(2,1)}, u32[]{:S(2)}) copy-start(bf16[48,48]{1,0:T(8,128)(2,1)} %param.10) | copy-start | bytes 13828
  117.3 94.4 %all-to-all-start.1 = ((f32[1,1,192,3072]{3,1,0,2:T(1,128)}), f32[1,1,192,3072]{3,1,0,2:T(1,128)}, u32[]{:S(2)}, u32[]{:S(2)}) async-start(f32[1,1,192,3072]{3,1,0,2:T(1,128)} %copy.25), calls=%async_computation.1 | async-start | bytes 4718592 | tf_op jit(solution)/shard_map/all_to_all | solution.py:62
  124.7 85.0 %all-gather.5.cloned.1.call-start = ((), (), s32[]{:S(2)}) async-start(), calls=%async_computation.4 | async-start | bytes 1597440 | tf_op jit(solution)/shard_map/all_gather | solution.py:41
  125.5 288.8 %all-reduce.5.cloned.1.call-start = ((), (), s32[]{:S(2)}) async-start(), calls=%async_computation.5 | async-start | bytes 2359296
  218.7 3.1 copy-start.2
Sparse Core Ops, SparseCore 0:
  27.6 82.5 all-gather.2
  129.4 80.2 all-gather.4
  218.9 195.4 all-reduce.4
where the time goes:
time: 673 us
  waiting for transfers between devices  345 us (51%)
  blocking collectives  264 us (39%)
  local copies, waits for them, and re-layouts  22.7 us (3%)
  between operations  14.6 us (2%)
  starting transfers between devices  12.1 us (2%)
  matrix products  11.2 us (2%)
    psum x1, blocking collectives, per_device(): grad_gates = lax.psum(partial_grad, 'etp')  249 us
    unnamed x4, waiting for transfers between devices  190 us
    all_gather x1, waiting for transfers between devices, per_device(): lax.all_gather(dy_recv, 'etp', axis=3, tiled=True)  82.1 us
    all_gather x1, waiting for transfers between devices, per_device(): lax.all_gather(x_recv, 'etp', axis=3, tiled=True)  73.1 us
    all_to_all x1, blocking collectives, per_device(): lax.all_to_all(x_sent, 'ep', split_axis=0, concat_axis=2, tiled=True)  14.6 us
  transfers between devices with their start and end apart: 5, of which 3 were waited for; matrix products, arithmetic and copies ran while one was open for 3% of the time, Pallas kernels for 0%

commit v1 on v0

--- a/solution.py
+++ b/solution.py
@@ -38,7 +38,9 @@
     )
     x_rows, dy_rows = (
         lax.all_gather(x_recv, "etp", axis=3, tiled=True),
-        lax.all_gather(dy_recv, "etp", axis=3, tiled=True),
+        jnp.concatenate(
+            lax.all_to_all(jnp.stack([dy_recv] * lax.axis_size("etp")), "etp", 0, 0), axis=3
+        ),
     )
     rows_x = x_rows[0]
     rows_dy = dy_rows[0]

time: 673 us -> 641 us (0.952)
  waiting for transfers between devices: 345 us -> 295 us
  blocking collectives: 264 us -> 274 us
  starting transfers between devices: 12.1 us -> 19.9 us
    all_gather x1 -> x0, waiting for transfers between devices: 82.1 us -> none  [per_device(): lax.all_gather(dy_recv, 'etp', axis=3, tiled=True)]
    all_to_all x1, waiting for transfers between devices: 0.01 us -> 53.3 us  [per_device(): lax.all_to_all(output_part[None], 'ep', split_axis=2, concat_axis=0, tile...]
    all_gather x1, waiting for transfers between devices: 73.1 us -> 55.5 us  [per_device(): lax.all_gather(x_recv, 'etp', axis=3, tiled=True)]
    all_to_all x0 -> x1, blocking collectives: none -> 10.2 us  [per_device(): lax.all_to_all(dy_sent, 'ep', split_axis=0, concat_axis=2, tiled=True)]
    all_to_all x1, starting transfers between devices: 4.64 us -> 13.1 us  [per_device(): lax.all_to_all(jnp.stack([dy_recv] * lax.axis_size('etp')), 'etp', 0, 0)]
    unnamed x4 -> x3, waiting for transfers between devices: 190 us -> 187 us
  transfers between devices with their start and end apart: 5 -> 4, of which waited for: 3 -> 3; matrix products, arithmetic and copies ran while one was open for 3% -> 3% of each run, Pallas kernels for 0% -> 0%
where the time goes in v1:
time: 641 us; the launch traced here: 640 us
  waiting for transfers between devices  295 us (46%)
  blocking collectives  274 us (43%)
  local copies, waits for them, and re-layouts  22.8 us (4%)
  starting transfers between devices  19.9 us (3%)
  between operations  14.9 us (2%)
  matrix products  9.8 us (2%)
    psum x1, blocking collectives, per_device(): grad_gates = lax.psum(partial_grad, 'etp')  249 us
    unnamed x3, waiting for transfers between devices  187 us
    all_gather x1, waiting for transfers between devices, per_device(): lax.all_gather(x_recv, 'etp', axis=3, tiled=True)  55.5 us
    all_to_all x1, waiting for transfers between devices, per_device(): lax.all_to_all(output_part[None], 'ep', split_axis=2, concat_axis=0, tile...  53.3 us
    all_to_all x1, blocking collectives, per_device(): lax.all_to_all(x_sent, 'ep', split_axis=0, concat_axis=2, tiled=True)  14.6 us
    all_to_all x1, starting transfers between devices, per_device(): lax.all_to_all(jnp.stack([dy_recv] * lax.axis_size('etp')), 'etp', 0, 0)  13.1 us
  transfers between devices with their start and end apart: 4, of which 3 were waited for; matrix products, arithmetic and copies ran while one was open for 3% of the time, Pallas kernels for 0%

profile of v1, /device:TPU:8, one launch (start us, length us, event | category | flops | bytes accessed | tf_op | source)
XLA Modules:
  0.0 639.9 jit_solution(4001386453044065437)
XLA Ops:
  7.2 0.7 broadcast_multiply_fusion
  8.0 0.8 copy.23
  8.7 0.1 copy.22
  8.8 0.1 mul.85
  9.0 0.1 eq.15
  9.1 0.1 fusion.17
  9.2 0.1 reduce_window_sum.11
  9.3 0.2 select_reduce_fusion
  9.5 0.9 scatter_custom_fusion
  10.4 0.7 concatenate.9
  11.1 0.8 gather_fusion
  11.9 0.1 reshape.219
  12.0 14.6 %all_to_all.35 = bf16[8,2,576]{2,1,0:T(2,128)(2,1)S(1)} all-to-all(bf16[8,2,576]{2,1,0:T(2,128)(2,1)S(1)} %reshape.219), channel_id=1, replica_groups=mesh['ep'=8,'etp'=64] {'ep'}, dimensions={0} | all-to-all | bytes 36864 | tf_op jit(solution)/shard_map/all_to_all | solution.py:36
  26.6 0.1 reshape.220
  26.7 0.7 copy.25
  27.5 0.8 copy.21
  28.2 0.7 concatenate.11
  28.9 0.8 gather_fusion.3
  29.7 0.1 reshape.167
  29.8 0.1 pad_maximum_fusion
  29.9 1.6 gather_fusion.2
  31.5 0.1 mul.92
  31.6 0.1 fusion.14
  31.7 0.1 reshape.221
  31.8 10.2 %all_to_all.36 = bf16[8,2,576]{2,1,0:T(2,128)(2,1)S(1)} all-to-all(bf16[8,2,576]{2,1,0:T(2,128)(2,1)S(1)} %reshape.221), channel_id=1, replica_groups=mesh['ep'=8,'etp'=64] {'ep'}, dimensions={0} | all-to-all | bytes 36864 | tf_op jit(solution)/shard_map/all_to_all | solution.py:37
  41.9 0.1 reshape.222
  42.1 0.1 copy.29
  42.2 1.3 stack.5
  43.4 13.1 %all-to-all-start.3 = ((bf16[64,1,1,192,48]{3,4,2,1,0:T(8,128)(2,1)}), bf16[64,1,1,192,48]{3,4,2,1,0:T(8,128)(2,1)S(1)}, u32[]{:S(2)}, u32[]{:S(2)}) async-start(bf16[64,1,1,192,48]{3,4,2,1,0:T(8,128)(2,1)} %stack.5), calls=%async_computation.3 | async-start | bytes 3145728 | tf_op jit(solution)/shard_map/all_to_all | solution.py:42
  56.5 55.5 %all-gather.2.cloned.1.call-done = bf16[1,1,192,3072]{2,3,1,0:T(8,128)(2,1)} async-done(((bf16[1,1,192,48]{2,3,1,0:T(8,128)(2,1)}), bf16[1,1,192,3072]{2,3,1,0:T(8,128)(2,1)}) %all-gather.2.cloned.1.call-update) | async-done | bytes 1179664 | tf_op jit(solution)/shard_map/all_gather | solution.py:40
  112.0 2.2 fusion.7
  114.2 0.6 multiply_convert_fusion.2
  114.8 0.5 convolution_bitcast_fusion
  115.3 3.8 copy.26
  119.1 6.8 %all-to-all-start.1 = ((f32[1,1,192,3072]{3,1,0,2:T(1,128)}), f32[1,1,192,3072]{3,1,0,2:T(1,128)}, u32[]{:S(2)}, u32[]{:S(2)}) async-start(f32[1,1,192,3072]{3,1,0,2:T(1,128)} %copy.26), calls=%async_computation.1 | async-start | bytes 4718592 | tf_op jit(solution)/shard_map/all_to_all | solution.py:64
  125.9 1.3 dynamic-slice
  127.9 0.6 fusion.9
  128.5 53.3 %all-to-all-done.1 = f32[1,1,192,3072]{3,1,0,2:T(1,128)} async-done(((f32[1,1,192,3072]{3,1,0,2:T(1,128)}), f32[1,1,192,3072]{3,1,0,2:T(1,128)}, u32[]{:S(2)}, u32[]{:S(2)}) %all-to-all-start.1) | async-done | bytes 2359328 | tf_op jit(solution)/shard_map/all_to_all | solution.py:64
  181.8 2.1 copy.35
  183.9 2.0 gather_fusion.1
  185.9 2.9 reshape.166
  188.8 3.1 fusion.2
  191.9 1.5 fusion.1
  193.4 1.5 fusion
  194.8 186.5 %all-reduce.5.cloned.1.call-done = f32[48,2,3072]{2,1,0:T(2,128)} async-done(((f32[48,2,3072]{2,1,0:T(2,128)}), f32[48,2,3072]{2,1,0:T(2,128)}) %all-reduce.5.cloned.1.call-update) | async-done | bytes 1179664
  381.3 1.7 multiply_reduce_fusion
  383.1 249.4 %psum.7 = f32[48,2]{1,0:T(8,128)S(1)} all-reduce(f32[48,2]{1,0:T(8,128)S(1)} %get-tuple-element.10), channel_id=1, replica_groups=mesh['ep'=8,'etp'=64] {'etp'}, use_global_device_ids=true, to_apply=%region_6.7 | all-reduce | flops 96 | bytes 768 | tf_op jit(solution)/shard_map/psum | solution.py:69
  632.4 0.6 copy.30
  (25 shorter events, 0.1 us)
Async XLA Ops:
  7.2 107.6 %copy-start = (bf16[1,128,3072]{2,1,0:T(8,128)(2,1)S(1)}, bf16[1,128,3072]{2,1,0:T(8,128)(2,1)}, u32[]{:S(2)}) copy-start(bf16[1,128,3072]{2,1,0:T(8,128)(2,1)} %param.13) | copy-start | bytes 2359300
  7.2 104.8 %all-gather.2.cloned.1.call-start = ((), (), s32[]{:S(2)}) async-start(), calls=%async_computation.4 | async-start | bytes 1597440 | tf_op jit(solution)/shard_map/all_gather | solution.py:40
  43.4 68.6 %copy-start.4 = (bf16[1,3072,128]{2,1,0:T(8,128)(2,1)S(1)}, bf16[1,3072,128]{2,1,0:T(8,128)(2,1)}, u32[]{:S(2)}) copy-start(bf16[1,3072,128]{2,1,0:T(8,128)(2,1)} %param.11) | copy-start | bytes 2359300
  43.4 75.7 %all-to-all-start.3 = ((bf16[64,1,1,192,48]{3,4,2,1,0:T(8,128)(2,1)}), bf16[64,1,1,192,48]{3,4,2,1,0:T(8,128)(2,1)S(1)}, u32[]{:S(2)}, u32[]{:S(2)}) async-start(bf16[64,1,1,192,48]{3,4,2,1,0:T(8,128)(2,1)} %stack.5), calls=%async_computation.3 | async-start | bytes 3145728 | tf_op jit(solution)/shard_map/all_to_all | solution.py:42
  112.0 2.2 copy-start.1
  112.0 2.2 copy-start.6
  119.1 6.8 %copy-start.5 = (bf16[48,48]{1,0:T(8,128)(2,1)S(1)}, bf16[48,48]{1,0:T(8,128)(2,1)}, u32[]{:S(2)}) copy-start(bf16[48,48]{1,0:T(8,128)(2,1)} %param.10) | copy-start | bytes 13828
  119.1 8.7 %copy-start.3 = (bf16[64,1,1,192,48]{3,4,2,1,0:T(8,128)(2,1)}, bf16[64,1,1,192,48]{3,4,2,1,0:T(8,128)(2,1)S(1)}, u32[]{:S(2)}) copy-start(bf16[64,1,1,192,48]{3,4,2,1,0:T(8,128)(2,1)S(1)} %all-to-all-done.3) | copy-start | bytes 3538948
  119.1 62.7 %all-to-all-start.1 = ((f32[1,1,192,3072]{3,1,0,2:T(1,128)}), f32[1,1,192,3072]{3,1,0,2:T(1,128)}, u32[]{:S(2)}, u32[]{:S(2)}) async-start(f32[1,1,192,3072]{3,1,0,2:T(1,128)} %copy.26), calls=%async_computation.1 | async-start | bytes 4718592 | tf_op jit(solution)/shard_map/all_to_all | solution.py:64
  125.9 255.4 %all-reduce.5.cloned.1.call-start = ((), (), s32[]{:S(2)}) async-start(), calls=%async_computation.5 | async-start | bytes 2359296
  188.8 3.1 copy-start.2
Sparse Core Ops, SparseCore 0:
  27.6 84.3 all-gather.1
  189.0 192.3 all-reduce.4
